TPU v7x, 32 devices: a whole 2x2x4 slice. The times are simulated.
32 devices in a mesh: groups: 2 (over y), head: 8 (over z, x), blk: 2 (over core).
Axes of the slice: x: 2, y: 2, z: 4, core: 2. Of those that a mesh axis runs over, the one named last changes fastest.
Arguments:
- queries: bfloat16 [256, 4096], P(('groups', 'head', 'blk')), parts along dimension 0, may hold values from -36 to 36
- keys: bfloat16 [256, 4096], P(('groups', 'head', 'blk')), parts along dimension 0, may hold values from -6 to 6
- values: bfloat16 [256, 4096], P(('groups', 'head', 'blk')), parts along dimension 0, may hold values from -12 to 12
- tile_mask: int32 [64, 1, 1], P('groups'), parts along dimension 0, may hold values from 0 to 1, as said below
Outputs:
- attended: bfloat16 [256, 4096], P(('groups', 'head', 'blk')), parts along dimension 0
There are 2 independent parts, one for each index of `groups`. A program takes and returns all parts, laid end to end along the dimension named above; each array names one. Nothing has to cross between parts.
Inputs may be any that keep to these rules, and one draw needn't show every extreme that they name: tile_mask[h, t, t] = 1 for every head h and query tile t.
All inputs are finite; a program needn't handle non-finite values.
Results may differ from a plain program's by a relative error of at most 0.005.
Values may be sent and summed in bfloat16 or wider, within the bound.
No kernel may reach another device: no remote copies, remote signals or barrier semaphores. Data moves between devices by JAX's collectives and lax.ppermute only.
A program may use at most 64 MiB of HBM per device.

v0:
```python
import jax
import jax.numpy as jnp
from jax import lax
from jax.sharding import PartitionSpec as P

H = 32
HD = 128
TILE = 128
big_negative = -1e30


def from_behind(array, axis, by):
    count = lax.axis_size(axis)
    return lax.ppermute(array, axis, [(i, (i + by) % count) for i in range(count)])


def update_block(inputs, k_rows, v_rows, k_tiles, heads_mask, score_scale):
    q_piece, q_tiles, out_sum, row_top, row_total = inputs
    rows_mask = jnp.take(heads_mask, q_tiles, axis=1)
    allowed = jnp.take(rows_mask, k_tiles, axis=2) > 0
    scores = (
        jnp.einsum("qhd,khd->hqk", q_piece, k_rows, preferred_element_type=jnp.float32)
        * score_scale
    )
    scores = jnp.where(allowed, scores, big_negative)
    new_top = jnp.maximum(row_top, jnp.max(scores, axis=2))
    factor = jnp.exp(row_top - new_top)
    weights = jnp.where(allowed, jnp.exp(scores - new_top[:, :, None]), 0.0)
    row_total = row_total * factor + jnp.sum(weights, axis=2)
    out_sum = out_sum * factor[:, :, None] + jnp.einsum(
        "hqk,khd->hqd", weights.astype(jnp.bfloat16), v_rows, preferred_element_type=jnp.float32
    )
    return (out_sum, new_top, row_total)


def attend(q_in, q_index, stacked, key_index_of, pass_on, heads_mask, per_dev, blk_count, my_blk):
    q_rows = q_in.reshape(-1, per_dev, HD)
    row_count = q_rows.shape[0]
    block_count = row_count // row_count
    q_blocks = q_rows.reshape(block_count, row_count, per_dev, HD)
    q_tiles = (q_index // TILE).reshape(block_count, row_count)
    out_sum = jnp.zeros((block_count, per_dev, row_count, HD), jnp.float32)
    row_top = jnp.full((block_count, per_dev, row_count), big_negative, jnp.float32)
    row_total = jnp.zeros((block_count, per_dev, row_count), jnp.float32)
    kv_pair = stacked
    for cycle_step in range(blk_count):
        if cycle_step > 0:
            kv_pair = pass_on(kv_pair)
        k_tiles = key_index_of((my_blk - cycle_step) % blk_count) // TILE
        k_rows = kv_pair[0].reshape(-1, per_dev, HD)
        v_rows = kv_pair[1].reshape(-1, per_dev, HD)

        def step_block(inputs):
            return update_block(inputs, k_rows, v_rows, k_tiles, heads_mask, HD ** (-0.5))

        out_sum, row_top, row_total = lax.map(
            step_block, (q_blocks, q_tiles, out_sum, row_top, row_total)
        )
    out_sum = out_sum.transpose(0, 2, 1, 3).reshape(row_count, per_dev, HD)
    row_top = row_top.transpose(0, 2, 1).reshape(row_count, per_dev)
    row_total = row_total.transpose(0, 2, 1).reshape(row_count, per_dev)
    return (out_sum, row_top, row_total)


def on_device(queries, keys, values, tile_mask):
    head_count = lax.axis_size("head")
    blk_count = lax.axis_size("blk")
    my_head = lax.axis_index("head")
    my_blk = lax.axis_index("blk")
    per_dev = max(1, H // head_count)
    split_count = max(1, head_count // H)
    groups = head_count // split_count
    row_width = per_dev * HD
    query_count = queries.shape[0]
    key_count = keys.shape[0]
    part_id = my_head % split_count
    heads_mask = lax.dynamic_slice_in_dim(tile_mask, my_head // split_count * per_dev, per_dev, 0)
    source = jnp.arange(head_count, dtype=jnp.int32)

    def copy_rows(matrix, row_count):
        shaped = matrix.reshape(row_count, groups, row_width).transpose(1, 0, 2)[:, None]
        return jnp.broadcast_to(shaped, (groups, split_count, row_count, row_width)).reshape(
            head_count, row_count, row_width
        )

    def index_of(per_source, offset, row_count, src_blk):
        starts = (source[:, None] * blk_count + src_blk) * per_source + offset
        return (starts + jnp.arange(row_count, dtype=jnp.int32)[None, :]).reshape(-1)

    sub_rows = query_count // split_count
    shaped = queries.reshape(split_count, query_count // split_count, groups, row_width)
    q_in = lax.all_to_all(
        shaped.transpose(2, 0, 1, 3).reshape(head_count, query_count // split_count, row_width),
        "head",
        split_axis=0,
        concat_axis=0,
        tiled=True,
    )
    k_in, v_in = (
        lax.all_to_all(copy_rows(keys, key_count), "head", split_axis=0, concat_axis=0, tiled=True),
        lax.all_to_all(
            copy_rows(values, key_count), "head", split_axis=0, concat_axis=0, tiled=True
        ),
    )
    kv_stack = jnp.stack([k_in, v_in])

    def pass_on(kv_pair):
        return from_behind(kv_pair, "blk", 1)

    def key_index_of(src_blk):
        return index_of(key_count, 0, key_count, src_blk)

    q_index = index_of(query_count, part_id * sub_rows, sub_rows, my_blk)
    out_sum, row_top, row_total = attend(
        q_in, q_index, kv_stack, key_index_of, pass_on, heads_mask, per_dev, blk_count, my_blk
    )
    result = (
        (out_sum / row_total[:, :, None])
        .astype(jnp.bfloat16)
        .reshape(head_count, sub_rows, row_width)
    )
    returned = lax.all_to_all(result, "head", split_axis=0, concat_axis=0, tiled=True)
    attended = (
        returned.reshape(groups, split_count, sub_rows, row_width)
        .transpose(1, 2, 0, 3)
        .reshape(query_count, H * HD)
    )
    return attended


def solution(mesh):
    in_specs = (
        P(("groups", "head", "blk"), None),
        P(("groups", "head", "blk"), None),
        P(("groups", "head", "blk"), None),
        P("groups", None, None),
    )
    out_specs = P(("groups", "head", "blk"), None)
    return jax.shard_map(
        on_device, mesh=mesh, in_specs=in_specs, out_specs=out_specs, check_vma=False
    )
```

profile of v0, /device:TPU:0, one launch (start us, length us, event | category | flops | bytes accessed | tf_op | source)
XLA Modules:
  0.0 46.3 jit_solution(11785490552753711157)
XLA Ops:
  0.0 0.0 copy-start
  0.0 7.4 %all-to-all-start.1 = ((bf16[8,8,512]{2,1,0:T(8,128)(2,1)}), bf16[8,8,512]{2,1,0:T(8,128)(2,1)S(1)}, u32[]{:S(2)}, u32[]{:S(2)}) async-start(bf16[8,8,512]{2,1,0:T(8,128)(2,1)} %bitcast.59), calls=%async_computation.1 | async-start | bytes 131072 | tf_op jit(solution)/shard_map/all_to_all | solution.py:100
  7.4 0.1 iota_add_fusion.2
  7.5 0.1 add.154
  7.6 0.1 iota_add_fusion.1
  7.7 0.1 add.161
  7.8 0.1 iota_add_fusion
  7.9 0.1 add.169
  8.0 0.0 copy-done
  8.0 0.1 dynamic-slice_bitcast_fusion
  8.0 0.1 select_bitcast_fusion
  8.1 6.2 %all-to-all-done.1 = bf16[8,8,512]{2,1,0:T(8,128)(2,1)S(1)} async-done(((bf16[8,8,512]{2,1,0:T(8,128)(2,1)}), bf16[8,8,512]{2,1,0:T(8,128)(2,1)S(1)}, u32[]{:S(2)}, u32[]{:S(2)}) %all-to-all-start.1) | async-done | bytes 65568 | tf_op jit(solution)/shard_map/all_to_all | solution.py:100
  14.3 3.4 %all-to-all-start.2 = ((bf16[8,8,512]{2,1,0:T(8,128)(2,1)}), bf16[8,8,512]{2,1,0:T(8,128)(2,1)S(1)}, u32[]{:S(2)}, u32[]{:S(2)}) async-start(bf16[8,8,512]{2,1,0:T(8,128)(2,1)} %bitcast.8), calls=%async_computation.2 | async-start | bytes 131072 | tf_op jit(solution)/shard_map/all_to_all | solution.py:101
  17.7 6.8 %all-to-all-done.2 = bf16[8,8,512]{2,1,0:T(8,128)(2,1)S(1)} async-done(((bf16[8,8,512]{2,1,0:T(8,128)(2,1)}), bf16[8,8,512]{2,1,0:T(8,128)(2,1)S(1)}, u32[]{:S(2)}, u32[]{:S(2)}) %all-to-all-start.2) | async-done | bytes 65568 | tf_op jit(solution)/shard_map/all_to_all | solution.py:101
  24.5 3.4 %all-to-all-start = ((bf16[8,8,512]{2,1,0:T(8,128)(2,1)}), bf16[8,8,512]{2,1,0:T(8,128)(2,1)S(1)}, u32[]{:S(2)}, u32[]{:S(2)}) async-start(bf16[8,8,512]{2,1,0:T(8,128)(2,1)} %bitcast.4), calls=%async_computation | async-start | bytes 131072 | tf_op jit(solution)/shard_map/all_to_all | solution.py:92
  27.9 0.1 collective-permute-start
  28.0 6.7 %all-to-all-done = bf16[8,8,512]{2,1,0:T(8,128)(2,1)S(1)} async-done(((bf16[8,8,512]{2,1,0:T(8,128)(2,1)}), bf16[8,8,512]{2,1,0:T(8,128)(2,1)S(1)}, u32[]{:S(2)}, u32[]{:S(2)}) %all-to-all-start) | async-done | bytes 65568 | tf_op jit(solution)/shard_map/all_to_all | solution.py:92
  34.7 0.2 fusion.46
  34.9 0.0 collective-permute-done
  35.0 0.2 fusion.45
  35.2 0.1 fusion.7
  35.4 0.3 fusion.3
  35.6 0.3 fusion
  35.9 0.1 copy.18
  36.0 0.1 reshape.168
  36.1 0.1 copy.19
  36.2 0.1 div.54
  36.3 0.1 div.55
  36.4 9.3 %all_to_all.20 = bf16[8,8,512]{2,1,0:T(8,128)(2,1)S(1)} all-to-all(bf16[8,8,512]{2,1,0:T(8,128)(2,1)S(1)} %divide_convert_fusion), channel_id=1, replica_groups=mesh['groups'=2,'head'=8,'blk'=2] {'head'}, dimensions={0} | all-to-all | bytes 131072 | tf_op jit(solution)/shard_map/all_to_all | solution.py:122
  45.7 0.6 %copy.43 = bf16[8,4096]{1,0:T(8,128)(2,1)} copy(bf16[8,4096]{1,0:T(8,128)(2,1)S(1)} %bitcast.58) | data formatting | bytes 131072
  (16 shorter events, 0.2 us)
Async XLA Ops:
  0.0 8.0 %copy-start = (s32[32,1,1]{0,2,1:T(1,128)S(1)}, s32[32,1,1]{0,2,1:T(1,128)}, u32[]{:S(2)}) copy-start(s32[32,1,1]{0,2,1:T(1,128)} %param.11) | copy-start | bytes 388
  0.0 14.3 %all-to-all-start.1 = ((bf16[8,8,512]{2,1,0:T(8,128)(2,1)}), bf16[8,8,512]{2,1,0:T(8,128)(2,1)S(1)}, u32[]{:S(2)}, u32[]{:S(2)}) async-start(bf16[8,8,512]{2,1,0:T(8,128)(2,1)} %bitcast.59), calls=%async_computation.1 | async-start | bytes 131072 | tf_op jit(solution)/shard_map/all_to_all | solution.py:100
  14.3 10.2 %all-to-all-start.2 = ((bf16[8,8,512]{2,1,0:T(8,128)(2,1)}), bf16[8,8,512]{2,1,0:T(8,128)(2,1)S(1)}, u32[]{:S(2)}, u32[]{:S(2)}) async-start(bf16[8,8,512]{2,1,0:T(8,128)(2,1)} %bitcast.8), calls=%async_computation.2 | async-start | bytes 131072 | tf_op jit(solution)/shard_map/all_to_all | solution.py:101
  24.5 10.2 %all-to-all-start = ((bf16[8,8,512]{2,1,0:T(8,128)(2,1)}), bf16[8,8,512]{2,1,0:T(8,128)(2,1)S(1)}, u32[]{:S(2)}, u32[]{:S(2)}) async-start(bf16[8,8,512]{2,1,0:T(8,128)(2,1)} %bitcast.4), calls=%async_computation | async-start | bytes 131072 | tf_op jit(solution)/shard_map/all_to_all | solution.py:92
  27.9 7.0 %collective-permute-start = (bf16[2,8,8,512]{3,2,1,0:T(8,128)(2,1)S(1)}, bf16[2,8,8,512]{3,2,1,0:T(8,128)(2,1)S(1)}, u32[]{:S(2)}, u32[]{:S(2)}) collective-permute-start(bf16[2,8,8,512]{3,2,1,0:T(8,128)(2,1)S(1)} %pad_maximum_fusion), channel_id=1, source_target_pairs={{0,1},{1,0},{2,3},{3,2},{4,5},{5,4},{6,7},{7,6},{8,9},{9,8},{10,11... | collective-permute-start | bytes 393224 | tf_op jit(solution)/shard_map/ppermute | solution.py:14
where the time goes:
time: 46.8 us; the launch traced here: 46.3 us
  waiting for transfers between devices  19.7 us (42%)
  starting transfers between devices  14.2 us (30%)
  blocking collectives  9.29 us (20%)
  local copies, waits for them, and re-layouts  1.49 us (3%)
  matrix products  0.94 us (2%)
  other arithmetic  0.55 us (1%)
    all_to_all x1, blocking collectives, on_device(): lax.all_to_all(result, 'head', split_axis=0, concat_axis=0, tiled=True)  9.29 us
    all_to_all x1, starting transfers between devices, on_device(): lax.all_to_all(copy_rows(keys, key_count), 'head', split_axis=0, concat_a...  7.41 us
    all_to_all x1, waiting for transfers between devices, on_device(): lax.all_to_all(copy_rows(values, key_count), 'head', split_axis=0, concat...  6.82 us
    all_to_all x1, waiting for transfers between devices, on_device(): lax.all_to_all(shaped.transpose(2, 0, 1, 3).reshape(head_count, query_cou...  6.69 us
    all_to_all x1, waiting for transfers between devices, on_device(): lax.all_to_all(copy_rows(keys, key_count), 'head', split_axis=0, concat_a...  6.19 us
    all_to_all x1, starting transfers between devices, on_device(): lax.all_to_all(copy_rows(values, key_count), 'head', split_axis=0, concat...  3.35 us
    all_to_all x1, starting transfers between devices, on_device(): lax.all_to_all(shaped.transpose(2, 0, 1, 3).reshape(head_count, query_cou...  3.35 us
  transfers between devices with their start and end apart: 4, of which 3 were waited for; matrix products, arithmetic and copies ran while one was open for 2% of the time, Pallas kernels for 0%

commit v1 on v0

--- a/solution.py
+++ b/solution.py
@@ -7,6 +7,28 @@
 HD = 128
 TILE = 128
 big_negative = -1e30
+
+
+def split_up(array, dim, length):
+    before, after = (array.shape[:dim], array.shape[dim + 1 :])
+    return jnp.moveaxis(array.reshape(*before, length, -1, *after), dim, 0)
+
+
+def in_order(tiles, dim):
+    tiles = jnp.moveaxis(tiles, 0, dim)
+    dims = tiles.shape
+    return tiles.reshape(*dims[:dim], dims[dim] * dims[dim + 1], *dims[dim + 2 :])
+
+
+def exchange_in_pairs(x, axis, split_dim, concat_dim):
+    count, index = (lax.axis_size(axis), lax.axis_index(axis))
+    pieces = split_up(x, split_dim, count)
+    outs = [pieces[index]]
+    for step in range(1, count):
+        sent = pieces[index ^ step]
+        outs.append(lax.ppermute(sent, axis, [(i, i ^ step) for i in range(count)]))
+    pieces = jnp.stack(outs)[index ^ jnp.arange(count)]
+    return in_order(pieces, concat_dim)
 
 
 def from_behind(array, axis, by):
@@ -119,7 +141,7 @@
         .astype(jnp.bfloat16)
         .reshape(head_count, sub_rows, row_width)
     )
-    returned = lax.all_to_all(result, "head", split_axis=0, concat_axis=0, tiled=True)
+    returned = exchange_in_pairs(result, "head", 0, 0)
     attended = (
         returned.reshape(groups, split_count, sub_rows, row_width)
         .transpose(1, 2, 0, 3)

time: 46.8 us -> 52.1 us (1.11)
  starting transfers between devices: 14.2 us -> 25.6 us
  blocking collectives: 9.29 us -> 0 us
  waiting for transfers between devices: 19.7 us -> 22 us
  local copies, waits for them, and re-layouts: 1.49 us -> 2.26 us
    ppermute x0 -> x7, starting transfers between devices: none -> 11.4 us  [exchange_in_pairs(): outs.append(lax.ppermute(sent, axis, [(i, i ^ step) for i in range(count)]))]
    all_to_all x1 -> x0, blocking collectives: 9.29 us -> none  [on_device(): lax.all_to_all(result, 'head', split_axis=0, concat_axis=0, tiled=True)]
    ppermute x0 -> x7, waiting for transfers between devices: none -> 2.28 us  [exchange_in_pairs(): outs.append(lax.ppermute(sent, axis, [(i, i ^ step) for i in range(count)]))]
    gather x0 -> x1, local copies, waits for them, and re-layouts: none -> 1.18 us  [exchange_in_pairs(): pieces = jnp.stack(outs)[index ^ jnp.arange(count)]]
  transfers between devices with their start and end apart: 4 -> 11, of which waited for: 3 -> 5; matrix products, arithmetic and copies ran while one was open for 2% -> 2% of each run, Pallas kernels for 0% -> 0%
where the time goes in v1:
time: 52.1 us; the launch traced here: 51.7 us
  starting transfers between devices  25.6 us (49%)
  waiting for transfers between devices  22 us (42%)
  local copies, waits for them, and re-layouts  2.26 us (4%)
  matrix products  0.94 us (2%)
  other arithmetic  0.66 us (1%)
    ppermute x7, starting transfers between devices, exchange_in_pairs(): outs.append(lax.ppermute(sent, axis, [(i, i ^ step) for i in range(count)]))  11.4 us
    all_to_all x1, starting transfers between devices, on_device(): lax.all_to_all(copy_rows(keys, key_count), 'head', split_axis=0, concat_a...  7.41 us
    all_to_all x1, waiting for transfers between devices, on_device(): lax.all_to_all(copy_rows(values, key_count), 'head', split_axis=0, concat...  6.77 us
    all_to_all x1, waiting for transfers between devices, on_device(): lax.all_to_all(shaped.transpose(2, 0, 1, 3).reshape(head_count, query_cou...  6.69 us
    all_to_all x1, waiting for transfers between devices, on_device(): lax.all_to_all(copy_rows(keys, key_count), 'head', split_axis=0, concat_a...  6.21 us
    all_to_all x1, starting transfers between devices, on_device(): lax.all_to_all(copy_rows(values, key_count), 'head', split_axis=0, concat...  3.35 us
    all_to_all x1, starting transfers between devices, on_device(): lax.all_to_all(shaped.transpose(2, 0, 1, 3).reshape(head_count, query_cou...  3.35 us
    ppermute x7, waiting for transfers between devices, exchange_in_pairs(): outs.append(lax.ppermute(sent, axis, [(i, i ^ step) for i in range(count)]))  2.28 us
  transfers between devices with their start and end apart: 11, of which 5 were waited for; matrix products, arithmetic and copies ran while one was open for 2% of the time, Pallas kernels for 0%

profile of v1, /device:TPU:0, one launch (start us, length us, event | category | flops | bytes accessed | tf_op | source)
XLA Modules:
  0.0 51.7 jit_solution(6219381288531490787)
XLA Ops:
  0.0 0.0 copy-start
  0.0 7.4 %all-to-all-start.1 = ((bf16[8,8,512]{2,1,0:T(8,128)(2,1)}), bf16[8,8,512]{2,1,0:T(8,128)(2,1)S(1)}, u32[]{:S(2)}, u32[]{:S(2)}) async-start(bf16[8,8,512]{2,1,0:T(8,128)(2,1)} %bitcast.96), calls=%async_computation.1 | async-start | bytes 131072 | tf_op jit(solution)/shard_map/all_to_all | solution.py:122
  7.5 0.1 iota_add_fusion.1
  7.5 0.1 add.195
  7.6 0.1 iota_add_fusion.2
  7.7 0.1 add.188
  7.8 0.1 iota_add_fusion
  7.9 0.1 add.203
  7.9 0.0 copy-done
  7.9 0.1 fusion.39
  8.0 0.1 select_bitcast_fusion
  8.1 6.2 %all-to-all-done.1 = bf16[8,8,512]{2,1,0:T(8,128)(2,1)S(1)} async-done(((bf16[8,8,512]{2,1,0:T(8,128)(2,1)}), bf16[8,8,512]{2,1,0:T(8,128)(2,1)S(1)}, u32[]{:S(2)}, u32[]{:S(2)}) %all-to-all-start.1) | async-done | bytes 65568 | tf_op jit(solution)/shard_map/all_to_all | solution.py:122
  14.3 3.4 %all-to-all-start.2 = ((bf16[8,8,512]{2,1,0:T(8,128)(2,1)}), bf16[8,8,512]{2,1,0:T(8,128)(2,1)S(1)}, u32[]{:S(2)}, u32[]{:S(2)}) async-start(bf16[8,8,512]{2,1,0:T(8,128)(2,1)} %bitcast.8), calls=%async_computation.2 | async-start | bytes 131072 | tf_op jit(solution)/shard_map/all_to_all | solution.py:123
  17.8 6.8 %all-to-all-done.2 = bf16[8,8,512]{2,1,0:T(8,128)(2,1)S(1)} async-done(((bf16[8,8,512]{2,1,0:T(8,128)(2,1)}), bf16[8,8,512]{2,1,0:T(8,128)(2,1)S(1)}, u32[]{:S(2)}, u32[]{:S(2)}) %all-to-all-start.2) | async-done | bytes 65568 | tf_op jit(solution)/shard_map/all_to_all | solution.py:123
  24.5 3.4 %all-to-all-start = ((bf16[8,8,512]{2,1,0:T(8,128)(2,1)}), bf16[8,8,512]{2,1,0:T(8,128)(2,1)S(1)}, u32[]{:S(2)}, u32[]{:S(2)}) async-start(bf16[8,8,512]{2,1,0:T(8,128)(2,1)} %bitcast.4), calls=%async_computation | async-start | bytes 131072 | tf_op jit(solution)/shard_map/all_to_all | solution.py:114
  27.9 0.1 collective-permute-start
  28.0 6.7 %all-to-all-done = bf16[8,8,512]{2,1,0:T(8,128)(2,1)S(1)} async-done(((bf16[8,8,512]{2,1,0:T(8,128)(2,1)}), bf16[8,8,512]{2,1,0:T(8,128)(2,1)S(1)}, u32[]{:S(2)}, u32[]{:S(2)}) %all-to-all-start) | async-done | bytes 65568 | tf_op jit(solution)/shard_map/all_to_all | solution.py:114
  34.7 0.2 fusion.48
  34.9 0.0 collective-permute-done
  35.0 0.2 fusion.47
  35.2 0.1 fusion.7
  35.4 0.3 fusion.3
  35.6 0.3 fusion
  35.9 0.1 copy.29
  36.0 0.1 copy.30
  36.1 0.1 div.60
  36.3 0.1 divide_convert_fusion
  36.4 0.2 constant_dynamic-slice_fusion
  36.6 0.5 collective-permute-start.1
  37.1 0.9 %collective-permute-start.2 = (bf16[1,8,512]{2,1,0:T(8,128)(2,1)S(1)}, bf16[1,8,512]{2,1,0:T(8,128)(2,1)S(1)}, u32[]{:S(2)}, u32[]{:S(2)}) collective-permute-start(bf16[1,8,512]{2,1,0:T(8,128)(2,1)S(1)} %bitcast.108), channel_id=1, source_target_pairs={{0,4},{2,6},{4,0},{6,2},{8,12},{10,14},{12,8},{14,10},{1,5},{3,7},... | collective-permute-start | bytes 24584 | tf_op jit(solution)/shard_map/ppermute | solution.py:29
  38.0 2.3 %collective-permute-start.3 = (bf16[1,8,512]{2,1,0:T(8,128)(2,1)S(1)}, bf16[1,8,512]{2,1,0:T(8,128)(2,1)S(1)}, u32[]{:S(2)}, u32[]{:S(2)}) collective-permute-start(bf16[1,8,512]{2,1,0:T(8,128)(2,1)S(1)} %bitcast.103), channel_id=1, source_target_pairs={{0,6},{2,4},{4,2},{6,0},{8,14},{10,12},{12,10},{14,8},{1,7},{3,5},... | collective-permute-start | bytes 24584 | tf_op jit(solution)/shard_map/ppermute | solution.py:29
  40.2 0.5 collective-permute-start.4
  40.7 2.3 %collective-permute-start.5 = (bf16[1,8,512]{2,1,0:T(8,128)(2,1)S(1)}, bf16[1,8,512]{2,1,0:T(8,128)(2,1)S(1)}, u32[]{:S(2)}, u32[]{:S(2)}) collective-permute-start(bf16[1,8,512]{2,1,0:T(8,128)(2,1)S(1)} %bitcast.99), channel_id=1, source_target_pairs={{0,10},{2,8},{4,14},{6,12},{8,2},{10,0},{12,6},{14,4},{1,11},{3,9}... | collective-permute-start | bytes 24584 | tf_op jit(solution)/shard_map/ppermute | solution.py:29
  43.0 0.0 collective-permute-done.1
  43.0 1.0 %collective-permute-start.6 = (bf16[1,8,512]{2,1,0:T(8,128)(2,1)S(1)}, bf16[1,8,512]{2,1,0:T(8,128)(2,1)S(1)}, u32[]{:S(2)}, u32[]{:S(2)}) collective-permute-start(bf16[1,8,512]{2,1,0:T(8,128)(2,1)S(1)} %bitcast.98), channel_id=1, source_target_pairs={{0,12},{2,14},{4,8},{6,10},{8,4},{10,6},{12,0},{14,2},{1,13},{3,15... | collective-permute-start | bytes 24584 | tf_op jit(solution)/shard_map/ppermute | solution.py:29
  44.1 0.0 collective-permute-done.2
  44.1 4.0 %collective-permute-start.7 = (bf16[1,8,512]{2,1,0:T(8,128)(2,1)S(1)}, bf16[1,8,512]{2,1,0:T(8,128)(2,1)S(1)}, u32[]{:S(2)}, u32[]{:S(2)}) collective-permute-start(bf16[1,8,512]{2,1,0:T(8,128)(2,1)S(1)} %bitcast.97), channel_id=1, source_target_pairs={{0,14},{2,12},{4,10},{6,8},{8,6},{10,4},{12,2},{14,0},{1,15},{3,13... | collective-permute-start | bytes 24584 | tf_op jit(solution)/shard_map/ppermute | solution.py:29
  48.1 0.0 collective-permute-done.3
  48.1 0.0 collective-permute-done.4
  48.2 0.0 collective-permute-done.5
  48.2 0.3 collective-permute-done.6
  48.6 1.9 %collective-permute-done.7 = bf16[1,8,512]{2,1,0:T(8,128)(2,1)S(1)} collective-permute-done((bf16[1,8,512]{2,1,0:T(8,128)(2,1)S(1)}, bf16[1,8,512]{2,1,0:T(8,128)(2,1)S(1)}, u32[]{:S(2)}, u32[]{:S(2)}) %collective-permute-start.7) | collective-permute-done | bytes 8224 | tf_op jit(solution)/shard_map/ppermute | solution.py:29
  50.5 1.2 %gather_fusion = bf16[8,8,512]{2,1,0:T(8,128)(2,1)} fusion(bf16[8,8,512]{2,1,0:T(8,128)(2,1)S(1)} %bitcast.95, s32[1024]{0:T(1024)S(1)} %pad_clamp_fusion), kind=kCustom, calls=%fused_computation | custom fusion | bytes 131104 | tf_op jit(solution)/shard_map/gather | solution.py:30
  (31 shorter events, 0.4 us)
Async XLA Ops:
  0.0 7.9 %copy-start = (s32[32,1,1]{0,2,1:T(1,128)S(1)}, s32[32,1,1]{0,2,1:T(1,128)}, u32[]{:S(2)}) copy-start(s32[32,1,1]{0,2,1:T(1,128)} %param.11) | copy-start | bytes 388
  0.0 14.3 %all-to-all-start.1 = ((bf16[8,8,512]{2,1,0:T(8,128)(2,1)}), bf16[8,8,512]{2,1,0:T(8,128)(2,1)S(1)}, u32[]{:S(2)}, u32[]{:S(2)}) async-start(bf16[8,8,512]{2,1,0:T(8,128)(2,1)} %bitcast.96), calls=%async_computation.1 | async-start | bytes 131072 | tf_op jit(solution)/shard_map/all_to_all | solution.py:122
  14.3 10.2 %all-to-all-start.2 = ((bf16[8,8,512]{2,1,0:T(8,128)(2,1)}), bf16[8,8,512]{2,1,0:T(8,128)(2,1)S(1)}, u32[]{:S(2)}, u32[]{:S(2)}) async-start(bf16[8,8,512]{2,1,0:T(8,128)(2,1)} %bitcast.8), calls=%async_computation.2 | async-start | bytes 131072 | tf_op jit(solution)/shard_map/all_to_all | solution.py:123
  24.5 10.2 %all-to-all-start = ((bf16[8,8,512]{2,1,0:T(8,128)(2,1)}), bf16[8,8,512]{2,1,0:T(8,128)(2,1)S(1)}, u32[]{:S(2)}, u32[]{:S(2)}) async-start(bf16[8,8,512]{2,1,0:T(8,128)(2,1)} %bitcast.4), calls=%async_computation | async-start | bytes 131072 | tf_op jit(solution)/shard_map/all_to_all | solution.py:114
  27.9 7.0 %collective-permute-start = (bf16[2,8,8,512]{3,2,1,0:T(8,128)(2,1)S(1)}, bf16[2,8,8,512]{3,2,1,0:T(8,128)(2,1)S(1)}, u32[]{:S(2)}, u32[]{:S(2)}) collective-permute-start(bf16[2,8,8,512]{3,2,1,0:T(8,128)(2,1)S(1)} %pad_maximum_fusion), channel_id=1, source_target_pairs={{0,1},{1,0},{2,3},{3,2},{4,5},{5,4},{6,7},{7,6},{8,9},{9,8},{10,11... | collective-permute-start | bytes 393224 | tf_op jit(solution)/shard_map/ppermute | solution.py:36
  36.6 6.4 %collective-permute-start.1 = (bf16[1,8,512]{2,1,0:T(8,128)(2,1)S(1)}, bf16[1,8,512]{2,1,0:T(8,128)(2,1)S(1)}, u32[]{:S(2)}, u32[]{:S(2)}) collective-permute-start(bf16[1,8,512]{2,1,0:T(8,128)(2,1)S(1)} %bitcast.110), channel_id=1, source_target_pairs={{0,2},{2,0},{4,6},{6,4},{8,10},{10,8},{12,14},{14,12},{1,3},{3,1},... | collective-permute-start | bytes 24584 | tf_op jit(solution)/shard_map/ppermute | solution.py:29
  37.1 7.0 %collective-permute-start.2 = (bf16[1,8,512]{2,1,0:T(8,128)(2,1)S(1)}, bf16[1,8,512]{2,1,0:T(8,128)(2,1)S(1)}, u32[]{:S(2)}, u32[]{:S(2)}) collective-permute-start(bf16[1,8,512]{2,1,0:T(8,128)(2,1)S(1)} %bitcast.108), channel_id=1, source_target_pairs={{0,4},{2,6},{4,0},{6,2},{8,12},{10,14},{12,8},{14,10},{1,5},{3,7},... | collective-permute-start | bytes 24584 | tf_op jit(solution)/shard_map/ppermute | solution.py:29
  38.0 10.1 %collective-permute-start.3 = (bf16[1,8,512]{2,1,0:T(8,128)(2,1)S(1)}, bf16[1,8,512]{2,1,0:T(8,128)(2,1)S(1)}, u32[]{:S(2)}, u32[]{:S(2)}) collective-permute-start(bf16[1,8,512]{2,1,0:T(8,128)(2,1)S(1)} %bitcast.103), channel_id=1, source_target_pairs={{0,6},{2,4},{4,2},{6,0},{8,14},{10,12},{12,10},{14,8},{1,7},{3,5},... | collective-permute-start | bytes 24584 | tf_op jit(solution)/shard_map/ppermute | solution.py:29
  40.2 7.9 %collective-permute-start.4 = (bf16[1,8,512]{2,1,0:T(8,128)(2,1)S(1)}, bf16[1,8,512]{2,1,0:T(8,128)(2,1)S(1)}, u32[]{:S(2)}, u32[]{:S(2)}) collective-permute-start(bf16[1,8,512]{2,1,0:T(8,128)(2,1)S(1)} %bitcast.101), channel_id=1, source_target_pairs={{0,8},{2,10},{4,12},{6,14},{8,0},{10,2},{12,4},{14,6},{1,9},{3,11}... | collective-permute-start | bytes 24584 | tf_op jit(solution)/shard_map/ppermute | solution.py:29
  40.7 7.4 %collective-permute-start.5 = (bf16[1,8,512]{2,1,0:T(8,128)(2,1)S(1)}, bf16[1,8,512]{2,1,0:T(8,128)(2,1)S(1)}, u32[]{:S(2)}, u32[]{:S(2)}) collective-permute-start(bf16[1,8,512]{2,1,0:T(8,128)(2,1)S(1)} %bitcast.99), channel_id=1, source_target_pairs={{0,10},{2,8},{4,14},{6,12},{8,2},{10,0},{12,6},{14,4},{1,11},{3,9}... | collective-permute-start | bytes 24584 | tf_op jit(solution)/shard_map/ppermute | solution.py:29
  43.0 5.5 %collective-permute-start.6 = (bf16[1,8,512]{2,1,0:T(8,128)(2,1)S(1)}, bf16[1,8,512]{2,1,0:T(8,128)(2,1)S(1)}, u32[]{:S(2)}, u32[]{:S(2)}) collective-permute-start(bf16[1,8,512]{2,1,0:T(8,128)(2,1)S(1)} %bitcast.98), channel_id=1, source_target_pairs={{0,12},{2,14},{4,8},{6,10},{8,4},{10,6},{12,0},{14,2},{1,13},{3,15... | collective-permute-start | bytes 24584 | tf_op jit(solution)/shard_map/ppermute | solution.py:29
  44.1 6.4 %collective-permute-start.7 = (bf16[1,8,512]{2,1,0:T(8,128)(2,1)S(1)}, bf16[1,8,512]{2,1,0:T(8,128)(2,1)S(1)}, u32[]{:S(2)}, u32[]{:S(2)}) collective-permute-start(bf16[1,8,512]{2,1,0:T(8,128)(2,1)S(1)} %bitcast.97), channel_id=1, source_target_pairs={{0,14},{2,12},{4,10},{6,8},{8,6},{10,4},{12,2},{14,0},{1,15},{3,13... | collective-permute-start | bytes 24584 | tf_op jit(solution)/shard_map/ppermute | solution.py:29
